TPU v7x, 32 devices: a whole 2x2x4 slice. The times are simulated.
32 devices in a mesh: ia: 4 (over z), ja: 2 (over y), ka: 4 (over x, core).
Axes of the slice: x: 2, y: 2, z: 4, core: 2. Of those that a mesh axis runs over, the one named last changes fastest.
Arguments:
- tile_values: bfloat16 [768, 128], P(('ia', 'ja', 'ka')), may hold values from -0.59765625 to 0.59765625
- tile_rows: int32 [768, 128], P(('ia', 'ja', 'ka')), may hold values from 0 to 63
- tile_cols: int32 [768, 128], P(('ia', 'ja', 'ka')), may hold values from 0 to 2047
- tile_depths: int32 [768, 128], P(('ia', 'ja', 'ka')), may hold values from 0 to 1023
- tile_live: int32 [32, 8], P(('ia', 'ja', 'ka')), may hold values from 0 to 3, as said below
- factor_b: bfloat16 [16, 2, 2048], P(None, 'ja', ('ia', 'ka')), may hold values from -6 to 6
- factor_c: bfloat16 [16, 4, 1024], P(None, 'ka', ('ia', 'ja')), may hold values from -6 to 6
- proj: float32 [16, 256], replicated, may hold values from -0.375 to 0.375
Outputs:
- tucker_y: float32 [2048, 256], P(('ia', 'ja', 'ka'))
- gram: float32 [256, 256], replicated
- new_factor: float32 [16, 2048], P(None, ('ia', 'ja', 'ka'))
Inputs may be any that keep to these rules, and one draw needn't show every extreme that they name: tile_live[d, o] counts the live leading slots among the 3 slots that device d holds for the device at index o along ja+ka within its mode-1 block; in every draw there is an owner for which every device has all 3 slots live, and every device has some owner with all 3 slots live.
All inputs are finite; a program needn't handle non-finite values.
Results may differ from a plain program's by a relative error of at most 0.0041.
Values may be sent and summed in bfloat16 or wider, within the bound.
A program may use at most 64 MiB of HBM per device.

v0:
```python
import jax
import jax.numpy as jnp
from jax import lax
from jax.sharding import PartitionSpec as P

RANK = 16
ROWS_DEV = 64


def owner_block(scaled, depth_rows, target):
    kron_rows = (scaled[:, None] * depth_rows[None, :]).reshape(
        scaled.shape[0] * depth_rows.shape[0], -1
    )
    onehot = (target.reshape(1, -1) == lax.iota(jnp.int32, ROWS_DEV)[:, None]).astype(jnp.bfloat16)
    return lax.dot_general(
        onehot, kron_rows, (((1,), (1,)), ((), ())), preferred_element_type=jnp.float32
    )


def group_blocks(scaled, depth_rows, target, begin_slot, pair_size, slot_count):
    rank_size = scaled.shape[0]
    tile_width = scaled.shape[2]
    scaled_part = lax.dynamic_slice_in_dim(scaled, begin_slot, pair_size * slot_count, 1)
    depth_part = lax.dynamic_slice_in_dim(depth_rows, begin_slot, pair_size * slot_count, 1)
    target_part = lax.dynamic_slice_in_dim(target, begin_slot, pair_size * slot_count, 0)
    scaled_part = scaled_part.reshape(rank_size, pair_size, slot_count, tile_width)
    depth_part = depth_part.reshape(depth_rows.shape[0], pair_size, slot_count, tile_width)
    target_part = target_part.reshape(pair_size, slot_count, tile_width)
    return jax.vmap(owner_block, in_axes=(1, 1, 0))(scaled_part, depth_part, target_part)


def owner_total(scaled, depth_rows, target, groups, slot_count):
    pair_size = 2
    columns = scaled.shape[0] * depth_rows.shape[0]
    result = jnp.zeros((ROWS_DEV, columns), jnp.float32)

    def turn(turn_index, result):
        begin_slot = turn_index * pair_size * slot_count
        blocks = group_blocks(scaled, depth_rows, target, begin_slot, pair_size, slot_count)
        return result + jnp.sum(blocks, axis=0)

    return lax.fori_loop(0, groups // pair_size, turn, result)


def on_device(tile_values, tile_rows, tile_cols, tile_depths, tile_live, factor_b, factor_c, proj):
    owners = lax.axis_size("ja") * lax.axis_size("ka")
    slot_total = tile_values.shape[0]
    slot_count = slot_total // owners
    mode_two = lax.all_gather(factor_b, ("ia", "ka"), axis=2, tiled=True)[:, 0, :]
    mode_three = lax.all_gather(factor_c, ("ia", "ja"), axis=2, tiled=True)[:, 0, :]
    slot_index = lax.iota(jnp.int32, slot_total)
    owner_of = slot_index // slot_count
    counts = jnp.sum(
        jnp.where(owner_of[:, None] == lax.iota(jnp.int32, owners)[None, :], tile_live, 0), axis=1
    )
    is_live = slot_index % slot_count < counts
    target = jnp.where(is_live[:, None], tile_rows, ROWS_DEV)
    scaled = (
        tile_values.astype(jnp.float32)[None]
        * jnp.take(mode_two, tile_cols, axis=1).astype(jnp.float32)
    ).astype(jnp.bfloat16)
    depth_rows = jnp.take(mode_three, tile_depths, axis=1)
    payload = jnp.concatenate([scaled, depth_rows], axis=0)
    arrived, routed = (
        lax.all_to_all(payload, ("ja", "ka"), split_axis=1, concat_axis=1, tiled=True),
        lax.all_to_all(target[None], ("ja", "ka"), split_axis=1, concat_axis=1, tiled=True),
    )
    summed = owner_total(arrived[:RANK], arrived[RANK:], routed[0], owners, slot_count)
    local_gram = lax.dot_general(
        summed,
        summed,
        (((0,), (0,)), ((), ())),
        precision=lax.Precision.HIGHEST,
        preferred_element_type=jnp.float32,
    )
    gram_total = lax.psum(local_gram, ("ia", "ja", "ka"))
    gram = gram_total / (ROWS_DEV * owners * lax.axis_size("ia"))
    new_factor = lax.dot_general(
        proj,
        summed,
        (((1,), (1,)), ((), ())),
        precision=lax.Precision.HIGHEST,
        preferred_element_type=jnp.float32,
    )
    return (summed, gram, new_factor)


def solution(mesh):
    return jax.shard_map(
        on_device,
        mesh=mesh,
        in_specs=(
            P(("ia", "ja", "ka"), None),
            P(("ia", "ja", "ka"), None),
            P(("ia", "ja", "ka"), None),
            P(("ia", "ja", "ka"), None),
            P(("ia", "ja", "ka"), None),
            P(None, "ja", ("ia", "ka")),
            P(None, "ka", ("ia", "ja")),
            P(),
        ),
        out_specs=(P(("ia", "ja", "ka"), None), P(), P(None, ("ia", "ja", "ka"))),
        check_vma=False,
    )
```

profile of v0, /device:TPU:0, one launch (start us, length us, event | category | flops | bytes accessed | tf_op | source)
XLA Modules:
  0.0 239.9 jit_solution(6678735856828618585)
XLA Ops:
  7.2 0.8 bitcast_clamp_fusion.1
  8.0 0.7 copy-done.3
  8.7 0.7 copy-done.6
  9.5 24.6 %all_gather.6 = bf16[16,1,2048]{0,2,1:T(8,128)(2,1)S(1)} all-gather(bf16[16,1,128]{0,2,1:T(8,128)(2,1)S(1)} %copy.29), channel_id=1, replica_groups=mesh['ia'=4,'ja'=2,'ka'=4] {'ia','ka'}, dimensions={2}, use_global_device_ids=true | all-gather | bytes 69632 | tf_op jit(solution)/shard_map/all_gather | solution.py:49
  34.1 9.2 %gather_fusion = bf16[3072,16]{1,0:T(8,128)(2,1)S(1)} fusion(bf16[16,2048]{0,1:T(8,128)(2,1)S(1)} %bitcast.41, s32[3072]{0:T(1024)S(1)} %bitcast_clamp_fusion.1), kind=kCustom, calls=%fused_computation | custom fusion | bytes 208896 | tf_op jit(solution)/shard_map/jit(_take)/gather | solution.py:60
  43.3 0.3 copy.30
  43.5 0.4 copy-done.5
  44.0 0.7 copy-done.7
  44.8 30.8 %all_gather.7 = bf16[16,1,1024]{0,2,1:T(8,128)(2,1)S(1)} all-gather(bf16[16,1,128]{0,2,1:T(8,128)(2,1)S(1)} %copy.31), channel_id=1, replica_groups=mesh['ia'=4,'ja'=2,'ka'=4] {'ia','ja'}, dimensions={2}, use_global_device_ids=true | all-gather | bytes 36864 | tf_op jit(solution)/shard_map/all_gather | solution.py:50
  75.5 9.2 %gather_fusion.1 = bf16[3072,16]{1,0:T(8,128)(2,1)S(1)} fusion(bf16[16,1024]{0,1:T(8,128)(2,1)S(1)} %bitcast.40, s32[3072]{0:T(1024)S(1)} %bitcast_clamp_fusion), kind=kCustom, calls=%fused_computation.1 | custom fusion | bytes 208896 | tf_op jit(solution)/shard_map/jit(_take)/gather | solution.py:62
  84.7 0.3 copy.32
  85.0 0.7 pad_maximum_fusion
  85.7 3.5 %all-to-all-start.1 = ((bf16[32,24,128]{2,0,1:T(8,128)(2,1)}), bf16[32,24,128]{2,0,1:T(8,128)(2,1)S(1)}, u32[]{:S(2)}, u32[]{:S(2)}) async-start(bf16[32,24,128]{2,0,1:T(8,128)(2,1)} %pad_maximum_fusion), calls=%async_computation.1 | async-start | bytes 393216 | tf_op jit(solution)/shard_map/all_to_all | solution.py:65
  89.3 0.6 copy-done.8
  90.1 0.7 broadcast_select_fusion
  90.7 4.7 %all-to-all-done.1 = bf16[32,24,128]{2,0,1:T(8,128)(2,1)S(1)} async-done(((bf16[32,24,128]{2,0,1:T(8,128)(2,1)}), bf16[32,24,128]{2,0,1:T(8,128)(2,1)S(1)}, u32[]{:S(2)}, u32[]{:S(2)}) %all-to-all-start.1) | async-done | bytes 196640 | tf_op jit(solution)/shard_map/all_to_all | solution.py:65
  95.4 3.3 %all-to-all-start = ((s32[1,24,128]{2,0,1:T(1,128)}), s32[1,24,128]{2,0,1:T(1,128)S(1)}, u32[]{:S(2)}, u32[]{:S(2)}) async-start(s32[1,24,128]{2,0,1:T(1,128)} %bitcast.1), calls=%async_computation | async-start | bytes 24576 | tf_op jit(solution)/shard_map/all_to_all | solution.py:66
  98.8 4.6 %all-to-all-done = s32[1,24,128]{2,0,1:T(1,128)S(1)} async-done(((s32[1,24,128]{2,0,1:T(1,128)}), s32[1,24,128]{2,0,1:T(1,128)S(1)}, u32[]{:S(2)}, u32[]{:S(2)}) %all-to-all-start) | async-done | bytes 12320 | tf_op jit(solution)/shard_map/all_to_all | solution.py:66
  103.4 3.7 %while.16 = (s32[]{:T(128)}, f32[64,256]{1,0:T(8,128)S(1)}, s32[24,128]{1,0:T(8,128)S(1)}, bf16[16,24,128]{2,0,1:T(8,128)(2,1)S(1)}, bf16[16,24,128]{2,0,1:T(8,1...) while((s32[]{:T(128)}, f32[64,256]{1,0:T(8,128)S(1)}, s32[24,128]{1,0:T(8,128)S(1)}, ...), condition=%wide.region_2.3_spmd.clone, body=%wide.region_1.2_spmd.clone.sunk | while | flops 25444360 | bytes 1965213 | solution.py:42
  103.7 0.3 mul.80
  104.0 0.3 fusion.14
  104.4 0.2 broadcast_multiply_fusion.3
  104.6 0.3 mul.80
  105.0 0.3 fusion.14
  105.5 0.3 mul.80
  105.9 0.3 fusion.14
  106.5 0.3 mul.80
  106.9 0.3 fusion.14
  107.2 1.1 fusion.5
  108.3 0.8 convolution_bitcast_fusion.1
  109.1 122.3 %all-reduce.2.cloned.1.call-done = f32[256,256]{1,0:T(8,128)} async-done(((f32[256,256]{1,0:T(8,128)}), f32[256,256]{1,0:T(8,128)}) %all-reduce.2.cloned.1.call-update) | async-done | bytes 262160 | tf_op jit(solution)/shard_map/psum | solution.py:76
  231.4 1.7 broadcast_multiply_fusion.1
  (51 shorter events, 1.4 us)
Async XLA Ops:
  7.2 101.2 %copy-start = (f32[16,256]{1,0:T(8,128)S(1)}, f32[16,256]{1,0:T(8,128)}, u32[]{:S(2)}) copy-start(f32[16,256]{1,0:T(8,128)} %param.17) | copy-start | bytes 49156
  7.2 0.8 copy-start.2
  8.0 0.7 copy-start.3
  8.7 0.7 copy-start.6
  43.3 0.7 copy-start.5
  44.0 0.7 copy-start.7
  85.7 4.3 %copy-start.4 = (s32[24,128]{1,0:T(8,128)S(1)}, s32[24,128]{1,0:T(8,128)}, u32[]{:S(2)}) copy-start(s32[24,128]{1,0:T(8,128)} %param.11) | copy-start | bytes 36868
  85.7 9.7 %all-to-all-start.1 = ((bf16[32,24,128]{2,0,1:T(8,128)(2,1)}), bf16[32,24,128]{2,0,1:T(8,128)(2,1)S(1)}, u32[]{:S(2)}, u32[]{:S(2)}) async-start(bf16[32,24,128]{2,0,1:T(8,128)(2,1)} %pad_maximum_fusion), calls=%async_computation.1 | async-start | bytes 393216 | tf_op jit(solution)/shard_map/all_to_all | solution.py:65
  89.3 0.7 copy-start.8
  95.4 8.0 %all-to-all-start = ((s32[1,24,128]{2,0,1:T(1,128)}), s32[1,24,128]{2,0,1:T(1,128)S(1)}, u32[]{:S(2)}, u32[]{:S(2)}) async-start(s32[1,24,128]{2,0,1:T(1,128)} %bitcast.1), calls=%async_computation | async-start | bytes 24576 | tf_op jit(solution)/shard_map/all_to_all | solution.py:66
  98.7 132.6 %all-reduce.2.cloned.1.call-start = ((), (), s32[]{:S(2)}) async-start(), calls=%async_computation.2 | async-start | bytes 524288 | tf_op jit(solution)/shard_map/psum | solution.py:76
  107.1 1.2 copy-start.1
Sparse Core Ops, SparseCore 0:
  108.4 122.8 all-reduce.1
where the time goes:
time: 240 us
  waiting for transfers between devices  132 us (55%)
  blocking collectives  55.4 us (23%)
  local copies, waits for them, and re-layouts  23.8 us (10%)
  between operations  14.2 us (6%)
  starting transfers between devices  6.9 us (3%)
  other arithmetic  4.78 us (2%)
  matrix products  2.99 us (1%)
    psum x1, waiting for transfers between devices, on_device(): gram_total = lax.psum(local_gram, ('ia', 'ja', 'ka'))  122 us
    all_gather x1, blocking collectives, on_device(): lax.all_gather(factor_c, ('ia', 'ja'), axis=2, tiled=True)[:, 0, :]  30.8 us
    all_gather x1, blocking collectives, on_device(): lax.all_gather(factor_b, ('ia', 'ka'), axis=2, tiled=True)[:, 0, :]  24.6 us
    gather x2, local copies, waits for them, and re-layouts, on_device(): depth_rows = jnp.take(mode_three, tile_depths, axis=1)  9.41 us
    gather x2, local copies, waits for them, and re-layouts, on_device(): jnp.take(mode_two, tile_cols, axis=1).astype(jnp.float32)  9.41 us
  transfers between devices with their start and end apart: 3, of which 3 were waited for; matrix products, arithmetic and copies ran while one was open for 1% of the time, Pallas kernels for 0%

commit v1 on v0

--- a/solution.py
+++ b/solution.py
@@ -73,7 +73,8 @@
         precision=lax.Precision.HIGHEST,
         preferred_element_type=jnp.float32,
     )
-    gram_total = lax.psum(local_gram, ("ia", "ja", "ka"))
+    terms = lax.all_gather(local_gram, ("ia", "ja", "ka"), axis=0, tiled=False)
+    gram_total = terms.sum(axis=0)
     gram = gram_total / (ROWS_DEV * owners * lax.axis_size("ia"))
     new_factor = lax.dot_general(
         proj,

time: 240 us -> 196 us (0.82)
  waiting for transfers between devices: 132 us -> 81.3 us
  other arithmetic: 4.78 us -> 11.9 us
    psum x1 -> x0, waiting for transfers between devices: 122 us -> none  [on_device(): gram_total = lax.psum(local_gram, ('ia', 'ja', 'ka'))]
    all_gather x0 -> x1, waiting for transfers between devices: none -> 72.7 us  [on_device(): terms = lax.all_gather(local_gram, ('ia', 'ja', 'ka'), axis=0, tiled=False)]
    reduce_sum x0 -> x1, other arithmetic: none -> 3.93 us  [on_device(): gram_total = terms.sum(axis=0)]
  transfers between devices with their start and end apart: 3 -> 3, of which waited for: 3 -> 3; matrix products, arithmetic and copies ran while one was open for 1% -> 2% of each run, Pallas kernels for 0% -> 0%
where the time goes in v1:
time: 196 us; the launch traced here: 195 us
  waiting for transfers between devices  81.3 us (41%)
  blocking collectives  55.4 us (28%)
  local copies, waits for them, and re-layouts  22 us (11%)
  between operations  14.1 us (7%)
  other arithmetic  11.9 us (6%)
  starting transfers between devices  6.77 us (3%)
  matrix products  2.99 us (2%)
    all_gather x1, waiting for transfers between devices, on_device(): terms = lax.all_gather(local_gram, ('ia', 'ja', 'ka'), axis=0, tiled=False)  72.7 us
    all_gather x1, blocking collectives, on_device(): lax.all_gather(factor_c, ('ia', 'ja'), axis=2, tiled=True)[:, 0, :]  30.8 us
    all_gather x1, blocking collectives, on_device(): lax.all_gather(factor_b, ('ia', 'ka'), axis=2, tiled=True)[:, 0, :]  24.6 us
    gather x2, local copies, waits for them, and re-layouts, on_device(): depth_rows = jnp.take(mode_three, tile_depths, axis=1)  9.41 us
    gather x2, local copies, waits for them, and re-layouts, on_device(): jnp.take(mode_two, tile_cols, axis=1).astype(jnp.float32)  9.41 us
    all_to_all x1, waiting for transfers between devices, on_device(): lax.all_to_all(target[None], ('ja', 'ka'), split_axis=1, concat_axis=1, t...  4.59 us
    all_to_all x1, waiting for transfers between devices, on_device(): lax.all_to_all(payload, ('ja', 'ka'), split_axis=1, concat_axis=1, tiled=...  3.98 us
    reduce_sum x1, other arithmetic, on_device(): gram_total = terms.sum(axis=0)  3.93 us
  transfers between devices with their start and end apart: 3, of which 3 were waited for; matrix products, arithmetic and copies ran while one was open for 2% of the time, Pallas kernels for 0%

profile of v1, /device:TPU:0, one launch (start us, length us, event | category | flops | bytes accessed | tf_op | source)
XLA Modules:
  0.0 194.8 jit_solution(6732461057492195418)
XLA Ops:
  7.2 0.7 bitcast_clamp_fusion.1
  7.9 0.7 compare_and_fusion.1
  8.6 0.7 bitcast_clamp_fusion
  9.3 0.7 compare_and_fusion
  10.0 0.8 copy.29
  10.8 24.6 %all_gather.12 = bf16[16,1,2048]{0,2,1:T(8,128)(2,1)S(1)} all-gather(bf16[16,1,128]{0,2,1:T(8,128)(2,1)S(1)} %copy.29), channel_id=1, replica_groups=mesh['ia'=4,'ja'=2,'ka'=4] {'ia','ka'}, dimensions={2}, use_global_device_ids=true | all-gather | bytes 69632 | tf_op jit(solution)/shard_map/all_gather | solution.py:49
  35.4 9.2 %gather_fusion = bf16[3072,16]{1,0:T(8,128)(2,1)S(1)} fusion(bf16[16,2048]{0,1:T(8,128)(2,1)S(1)} %bitcast.43, s32[3072]{0:T(1024)S(1)} %bitcast_clamp_fusion.1), kind=kCustom, calls=%fused_computation | custom fusion | bytes 208896 | tf_op jit(solution)/shard_map/jit(_take)/gather | solution.py:60
  44.9 0.7 convert_element_type.12
  45.6 0.8 copy.31
  46.4 30.8 %all_gather.13 = bf16[16,1,1024]{0,2,1:T(8,128)(2,1)S(1)} all-gather(bf16[16,1,128]{0,2,1:T(8,128)(2,1)S(1)} %copy.31), channel_id=1, replica_groups=mesh['ia'=4,'ja'=2,'ka'=4] {'ia','ja'}, dimensions={2}, use_global_device_ids=true | all-gather | bytes 36864 | tf_op jit(solution)/shard_map/all_gather | solution.py:50
  77.1 9.2 %gather_fusion.1 = bf16[3072,16]{1,0:T(8,128)(2,1)S(1)} fusion(bf16[16,1024]{0,1:T(8,128)(2,1)S(1)} %bitcast.42, s32[3072]{0:T(1024)S(1)} %bitcast_clamp_fusion), kind=kCustom, calls=%fused_computation.1 | custom fusion | bytes 208896 | tf_op jit(solution)/shard_map/jit(_take)/gather | solution.py:62
  86.6 0.7 pad_maximum_fusion
  87.3 3.4 %all-to-all-start.1 = ((bf16[32,24,128]{2,0,1:T(8,128)(2,1)}), bf16[32,24,128]{2,0,1:T(8,128)(2,1)S(1)}, u32[]{:S(2)}, u32[]{:S(2)}) async-start(bf16[32,24,128]{2,0,1:T(8,128)(2,1)} %pad_maximum_fusion), calls=%async_computation.1 | async-start | bytes 393216 | tf_op jit(solution)/shard_map/all_to_all | solution.py:65
  90.8 0.7 select_reduce_fusion
  91.5 1.4 broadcast_select_fusion
  92.9 4.0 %all-to-all-done.1 = bf16[32,24,128]{2,0,1:T(8,128)(2,1)S(1)} async-done(((bf16[32,24,128]{2,0,1:T(8,128)(2,1)}), bf16[32,24,128]{2,0,1:T(8,128)(2,1)S(1)}, u32[]{:S(2)}, u32[]{:S(2)}) %all-to-all-start.1) | async-done | bytes 196640 | tf_op jit(solution)/shard_map/all_to_all | solution.py:65
  96.9 3.3 %all-to-all-start = ((s32[1,24,128]{2,0,1:T(1,128)}), s32[1,24,128]{2,0,1:T(1,128)S(1)}, u32[]{:S(2)}, u32[]{:S(2)}) async-start(s32[1,24,128]{2,0,1:T(1,128)} %bitcast.1), calls=%async_computation | async-start | bytes 24576 | tf_op jit(solution)/shard_map/all_to_all | solution.py:66
  100.3 4.6 %all-to-all-done = s32[1,24,128]{2,0,1:T(1,128)S(1)} async-done(((s32[1,24,128]{2,0,1:T(1,128)}), s32[1,24,128]{2,0,1:T(1,128)S(1)}, u32[]{:S(2)}, u32[]{:S(2)}) %all-to-all-start) | async-done | bytes 12320 | tf_op jit(solution)/shard_map/all_to_all | solution.py:66
  104.9 3.7 %while.16 = (s32[]{:T(128)}, f32[64,256]{1,0:T(8,128)S(1)}, s32[24,128]{1,0:T(8,128)S(1)}, bf16[16,24,128]{2,0,1:T(8,128)(2,1)S(1)}, bf16[16,24,128]{2,0,1:T(8,1...) while((s32[]{:T(128)}, f32[64,256]{1,0:T(8,128)S(1)}, s32[24,128]{1,0:T(8,128)S(1)}, ...), condition=%wide.region_2.3_spmd.clone, body=%wide.region_1.2_spmd.clone.sunk | while | flops 25444360 | bytes 1965213 | solution.py:42
  105.1 0.3 mul.80
  105.5 0.3 fusion.14
  106.1 0.3 mul.80
  106.5 0.3 fusion.14
  107.0 0.3 mul.80
  107.4 0.3 fusion.14
  108.0 0.3 mul.80
  108.3 0.3 fusion.14
  108.6 1.1 fusion.5
  109.8 0.8 convolution_bitcast_fusion.1
  110.6 72.7 %all-gather.3.cloned.1.call-done = f32[8192,256]{1,0:T(8,128)} async-done(((f32[256,256]{1,0:T(8,128)}), f32[8192,256]{1,0:T(8,128)}) %all-gather.3.cloned.1.call-update) | async-done | bytes 8388624 | tf_op jit(solution)/shard_map/all_gather | solution.py:76
  183.3 3.9 %reduce_sum.25 = f32[256,256]{1,0:T(8,128)S(1)} reduce(f32[32,256,256]{2,1,0:T(8,128)} %bitcast.41, f32[]{:T(128)} %constant.98.clone.1), dimensions={0}, to_apply=%region_3.4 | reduce | flops 2031616 | bytes 8650756 | tf_op jit(solution)/shard_map/reduce_sum | solution.py:77
  187.2 0.7 broadcast_multiply_fusion.1
  (38 shorter events, 1.7 us)
Async XLA Ops:
  7.2 102.6 %copy-start = (f32[16,256]{1,0:T(8,128)S(1)}, f32[16,256]{1,0:T(8,128)}, u32[]{:S(2)}) copy-start(f32[16,256]{1,0:T(8,128)} %param.17) | copy-start | bytes 49156
  87.3 9.5 %all-to-all-start.1 = ((bf16[32,24,128]{2,0,1:T(8,128)(2,1)}), bf16[32,24,128]{2,0,1:T(8,128)(2,1)S(1)}, u32[]{:S(2)}, u32[]{:S(2)}) async-start(bf16[32,24,128]{2,0,1:T(8,128)(2,1)} %pad_maximum_fusion), calls=%async_computation.1 | async-start | bytes 393216 | tf_op jit(solution)/shard_map/all_to_all | solution.py:65
  96.9 8.0 %all-to-all-start = ((s32[1,24,128]{2,0,1:T(1,128)}), s32[1,24,128]{2,0,1:T(1,128)S(1)}, u32[]{:S(2)}, u32[]{:S(2)}) async-start(s32[1,24,128]{2,0,1:T(1,128)} %bitcast.1), calls=%async_computation | async-start | bytes 24576 | tf_op jit(solution)/shard_map/all_to_all | solution.py:66
  100.2 83.1 %all-gather.3.cloned.1.call-start = ((), (), s32[]{:S(2)}) async-start(), calls=%async_computation.2 | async-start | bytes 8650752 | tf_op jit(solution)/shard_map/all_gather | solution.py:76
  108.6 79.3 %copy-start.1 = (f32[64,256]{1,0:T(8,128)}, f32[64,256]{1,0:T(8,128)S(1)}, u32[]{:S(2)}) copy-start(f32[64,256]{1,0:T(8,128)S(1)} %get-tuple-element.132) | copy-start | bytes 196612
Sparse Core Ops, SparseCore 0:
  109.9 73.3 all-gather.2
